TPU v7x, 32 devices: a whole 2x2x4 slice. The times are simulated.
32 devices in a mesh: query: 8 (over z, y), store: 4 (over x, core).
Axes of the slice: x: 2, y: 2, z: 4, core: 2. Of those that a mesh axis runs over, the one named last changes fastest.
Arguments:
- in_rows: bfloat16 [8, 16384, 64], P('query', 'store'), may hold values from -6 to 6
- out_rows: bfloat16 [8, 16384, 128], P('query', 'store'), may hold values from -0.625 to 0.625
- row_doc: int32 [8, 16384], P('query', 'store'), may hold values from 0 to 31
- row_pos: int32 [8, 16384], P('query', 'store'), may hold values from 0 to 255
- doc_len: int32 [8, 128], P('query', 'store'), may hold values from 128 to 256
- eig_in: float32 [64], replicated, may hold values from 0.25 to 2
- eig_out: float32 [128], replicated, may hold values from 0.25 to 2
- basis_in: float32 [64, 64], replicated, may hold values from -0.75 to 0.75
- basis_out: float32 [128, 128], replicated, may hold values from -0.5 to 0.5
- train_feats: bfloat16 [8, 768, 8192], P('query', 'store'), may hold values from -0.0625 to 0.0625
Outputs:
- scores: bfloat16 [8, 128, 768], P('query', None, 'store')
Inputs may be any that keep to these rules, and one draw needn't show every extreme that they name: On each device the 4096 rows form 8 blocks of 512 rows in order; the rows of block j belong to documents of group j in the same store column, and row_doc names the document among that destination's 32.
All inputs are finite; a program needn't handle non-finite values.
Results may differ from a plain program's by a relative error of at most 0.0049.
Values may be sent and summed in bfloat16 or wider, within the bound.
A program may use at most 64 MiB of HBM per device.

v0:
```python
import math
import jax
import jax.numpy as jnp
from jax import lax
from jax.sharding import PartitionSpec as P

damping = 0.1
highest = lax.Precision.HIGHEST


def from_behind(x, axis, by):
    devices = lax.axis_size(axis)
    return lax.ppermute(x, axis, [(i, (i + by) % devices) for i in range(devices)])


def precondition(gradients, scaling, basis_in, basis_out):
    in_width = basis_in.shape[0]
    out_width = basis_out.shape[0]
    doc_count = gradients.shape[1] // in_width
    rotated = jnp.dot(basis_out.T, gradients, precision=highest)
    turned = jnp.dot(rotated.reshape(out_width * doc_count, in_width), basis_in, precision=highest)
    turned = turned.reshape(out_width, doc_count, in_width) * scaling[:, None, :]
    restored = jnp.dot(
        basis_out, turned.reshape(out_width, doc_count * in_width), precision=highest
    )
    final_map = jnp.dot(
        restored.reshape(out_width * doc_count, in_width), basis_in.T, precision=highest
    )
    final_map = final_map.reshape(out_width, doc_count, in_width)
    return (
        jnp.transpose(final_map, (1, 0, 2))
        .reshape(doc_count, out_width * in_width)
        .astype(jnp.bfloat16)
    )


def record(score_table, query_block, anchor, train_slab):
    partial_scores = lax.dot_general(
        query_block, train_slab, (((1,), (1,)), ((), ())), preferred_element_type=jnp.float32
    )
    return lax.dynamic_update_slice_in_dim(
        score_table, partial_scores.astype(jnp.bfloat16), anchor * query_block.shape[0], 0
    )


def on_device(
    in_rows, out_rows, row_doc, row_pos, doc_len, eig_in, eig_out, basis_in, basis_out, train_feats
):
    doc_count = doc_len.shape[1]
    in_width = in_rows.shape[2]
    packed_keys = row_doc * 65536 + row_pos
    inputs_side, grads_side, keys_side = (
        lax.all_to_all(in_rows, "query", split_axis=1, concat_axis=1, tiled=True),
        lax.all_to_all(out_rows, "query", split_axis=1, concat_axis=1, tiled=True),
        lax.all_to_all(packed_keys, "query", split_axis=1, concat_axis=1, tiled=True),
    )
    inputs_side = inputs_side[0]
    grads_side = grads_side[0]
    keys_side = keys_side[0]
    doc_of_row = keys_side // 65536
    pos_of_row = keys_side % 65536
    live_mask = (doc_of_row[:, None] == jnp.arange(doc_count, dtype=jnp.int32)[None, :]) & (
        pos_of_row[:, None] < doc_len[0][None, :]
    )
    weights = live_mask.astype(jnp.bfloat16)
    row_count = inputs_side.shape[0]
    row_span = math.gcd(row_count, 1024)

    def accumulate(turn_index, running):
        row_start = turn_index * row_span
        x_part = lax.dynamic_slice_in_dim(inputs_side, row_start, row_span, 0)
        g_part = lax.dynamic_slice_in_dim(grads_side, row_start, row_span, 0)
        w_part = lax.dynamic_slice_in_dim(weights, row_start, row_span, 0)
        spread = (w_part[:, :, None] * x_part[:, None, :]).reshape(row_span, doc_count * in_width)
        return running + lax.dot_general(
            g_part, spread, (((0,), (0,)), ((), ())), preferred_element_type=jnp.float32
        )

    gradients = jnp.zeros((grads_side.shape[1], doc_count * in_width), jnp.float32)
    gradients = lax.fori_loop(0, row_count // row_span, accumulate, gradients)
    scaling = 1.0 / (eig_out[:, None] * eig_in[None, :] + damping)
    query_block = precondition(gradients, scaling, basis_in, basis_out)
    train_slab = train_feats[0]
    store_count = lax.axis_size("store")
    own_index = lax.axis_index("store")
    score_table = jnp.zeros((store_count * doc_count, train_slab.shape[0]), jnp.bfloat16)

    def travel(carry, visit_index):
        moving, table_now = carry
        table_now = record(table_now, moving, (own_index - visit_index) % store_count, train_slab)
        moving = from_behind(moving, "store", 1)
        return ((moving, table_now), None)

    (moving, score_table), _ = lax.scan(
        travel, (query_block, score_table), jnp.arange(store_count - 1, dtype=jnp.int32)
    )
    score_table = record(
        score_table, moving, (own_index - (store_count - 1)) % store_count, train_slab
    )
    return score_table[None]


def solution(mesh):
    placed = (
        P("query", "store", None),
        P("query", "store", None),
        P("query", "store"),
        P("query", "store"),
        P("query", "store"),
        P(),
        P(),
        P(),
        P(),
        P("query", "store", None),
    )
    return jax.shard_map(
        on_device, mesh=mesh, in_specs=placed, out_specs=P("query", None, "store"), check_vma=False
    )
```

profile of v0, /device:TPU:0, one launch (start us, length us, event | category | flops | bytes accessed | tf_op | source)
XLA Modules:
  0.0 183.5 jit_solution(18066739965186172153)
XLA Ops:
  1.4 7.3 %all-to-all-start.1 = ((s32[1,8,512]{2,0,1:T(1,128)}), s32[1,8,512]{2,0,1:T(1,128)S(1)}, u32[]{:S(2)}, u32[]{:S(2)}) async-start(s32[1,8,512]{2,0,1:T(1,128)} %bitcast.1), calls=%async_computation.1 | async-start | bytes 32768 | tf_op jit(solution)/shard_map/all_to_all | solution.py:55
  8.7 4.9 %copy.27 = bf16[1,4096,64]{2,0,1:T(2,128)(2,1)S(1)} copy(bf16[1,4096,64]{1,2,0:T(8,128)(2,1)} %param.14) | data formatting | bytes 1048576 | tf_op args[0]
  14.1 22.3 %reduce.1 = bf16[4096,64]{1,0:T(8,128)(2,1)S(1)} reduce(bf16[4096,1,64]{2,1,0:T(2,128)(2,1)S(1)} %bitcast.60, bf16[]{:T(256)} %broadcast.96), dimensions={1}, to_apply=%bitcast.31.reduce_sub_computation | reduce | bytes 1048578
  37.9 6.0 %all-to-all-start.2 = ((bf16[8,2,16384]{2,1,0:T(2,128)(2,1)}), bf16[8,2,16384]{2,1,0:T(2,128)(2,1)}, u32[]{:S(2)}, u32[]{:S(2)}) async-start(bf16[8,2,16384]{2,1,0:T(2,128)(2,1)} %reshape.110), calls=%async_computation.2 | async-start | bytes 1048576 | tf_op jit(solution)/shard_map/all_to_all | solution.py:53
  43.9 3.2 %copy.39 = bf16[1,4096,128]{2,0,1:T(2,128)(2,1)S(1)} copy(bf16[1,4096,128]{2,1,0:T(8,128)(2,1)} %param.15) | data formatting | bytes 2097152 | tf_op args[1]
  47.1 22.3 %reduce = bf16[4096,128]{1,0:T(8,128)(2,1)S(1)} reduce(bf16[4096,1,128]{2,1,0:T(2,128)(2,1)S(1)} %bitcast.62, bf16[]{:T(256)} %broadcast.96), dimensions={1}, to_apply=%bitcast.45.reduce_sub_computation | reduce | bytes 2097154
  70.6 6.0 %all-to-all-start = ((bf16[8,2,32768]{2,1,0:T(2,128)(2,1)}), bf16[8,2,32768]{2,1,0:T(2,128)(2,1)}, u32[]{:S(2)}, u32[]{:S(2)}) async-start(bf16[8,2,32768]{2,1,0:T(2,128)(2,1)} %reshape.108), calls=%async_computation | async-start | bytes 2097152 | tf_op jit(solution)/shard_map/all_to_all | solution.py:54
  76.9 4.1 %reshape.111 = bf16[4096,1,64]{2,1,0:T(2,128)(2,1)S(1)} reshape(bf16[8,2,16384]{2,1,0:T(2,128)(2,1)} %all-to-all-done.2) | data formatting | bytes 1048576
  81.0 3.6 %copy.28 = bf16[1,4096,64]{1,2,0:T(8,128)(2,1)} copy(bf16[1,4096,64]{2,0,1:T(2,128)(2,1)S(1)} %bitcast.59) | data formatting | bytes 1048576 | tf_op jit(solution)/shard_map/all_to_all | solution.py:53
  84.7 16.9 %all-to-all-done = bf16[8,2,32768]{2,1,0:T(2,128)(2,1)} async-done(((bf16[8,2,32768]{2,1,0:T(2,128)(2,1)}), bf16[8,2,32768]{2,1,0:T(2,128)(2,1)}, u32[]{:S(2)}, u32[]{:S(2)}) %all-to-all-start) | async-done | bytes 1048608 | tf_op jit(solution)/shard_map/all_to_all | solution.py:54
  101.5 4.3 %reshape.109 = bf16[4096,1,128]{2,1,0:T(2,128)(2,1)S(1)} reshape(bf16[8,2,32768]{2,1,0:T(2,128)(2,1)} %all-to-all-done) | data formatting | bytes 2097152
  107.0 28.7 %while.29 = (s32[]{:T(128)}, f32[128,2048]{1,0:T(8,128)S(1)}, bf16[4096,128]{1,0:T(8,128)(2,1)}, bf16[4096,32]{0,1:T(8,128)(2,1)S(1)}, bf16[4096,64]{0,1:T(8,128...) while((s32[]{:T(128)}, f32[128,2048]{1,0:T(8,128)S(1)}, bf16[4096,128]{1,0:T(8,128)(2,1)}, ...), condition=%wide.region_1.2_spmd.clone, body=%wide.region_0.1_spmd.clone.sunk | while | flops 539492352 | bytes 11337897 | solution.py:80
  107.9 2.2 %broadcast_multiply_fusion.2 = bf16[1024,32,64]{0,2,1:T(8,128)(2,1)} fusion(bf16[1024,64]{0,1:T(8,128)(2,1)S(1)} %constant_dynamic-slice_fusion.4, bf16[1024,32]{0,1:T(8,128)(2,1)S(1)} %constant_dynamic-slice_fusion.5), kind=kLoop, calls=%fused_computation.3.clone.1 | loop fusion | flops 2097152 | bytes 4390912 | tf_op jit(solution)/shard_map/while/body/eval_jaxpr/mul | solution.py:74
  110.1 4.0 %convolution_add_fusion.2 = f32[128,2048]{1,0:T(8,128)S(1)} fusion(bf16[1024,2048]{0,1:T(8,128)(2,1)} %bitcast.56, f32[128,2048]{1,0:T(8,128)S(1)} %get-tuple-element.306, pred[]{:T(512)S(6)} %compare.16, bf16[4096,128]{1,0:T(8,128)(2,1)} %get-tuple-element.316, s32[]{:T(128)S(6)} %select_n.65), kind=kOutput, calls=%fused_computation.2.clone.1 | convolution fusion | flops 537395200 | bytes 6553605 | tf_op jit(solution)/shard_map/while/body/eval_jaxpr/dot_general | solution.py:75
  115.1 2.2 %broadcast_multiply_fusion.2 = bf16[1024,32,64]{0,2,1:T(8,128)(2,1)} fusion(bf16[1024,64]{0,1:T(8,128)(2,1)S(1)} %constant_dynamic-slice_fusion.4, bf16[1024,32]{0,1:T(8,128)(2,1)S(1)} %constant_dynamic-slice_fusion.5), kind=kLoop, calls=%fused_computation.3.clone.1 | loop fusion | flops 2097152 | bytes 4390912 | tf_op jit(solution)/shard_map/while/body/eval_jaxpr/mul | solution.py:74
  117.3 4.0 %convolution_add_fusion.2 = f32[128,2048]{1,0:T(8,128)S(1)} fusion(bf16[1024,2048]{0,1:T(8,128)(2,1)} %bitcast.56, f32[128,2048]{1,0:T(8,128)S(1)} %get-tuple-element.306, pred[]{:T(512)S(6)} %compare.16, bf16[4096,128]{1,0:T(8,128)(2,1)} %get-tuple-element.316, s32[]{:T(128)S(6)} %select_n.65), kind=kOutput, calls=%fused_computation.2.clone.1 | convolution fusion | flops 537395200 | bytes 6553605 | tf_op jit(solution)/shard_map/while/body/eval_jaxpr/dot_general | solution.py:75
  122.3 2.2 %broadcast_multiply_fusion.2 = bf16[1024,32,64]{0,2,1:T(8,128)(2,1)} fusion(bf16[1024,64]{0,1:T(8,128)(2,1)S(1)} %constant_dynamic-slice_fusion.4, bf16[1024,32]{0,1:T(8,128)(2,1)S(1)} %constant_dynamic-slice_fusion.5), kind=kLoop, calls=%fused_computation.3.clone.1 | loop fusion | flops 2097152 | bytes 4390912 | tf_op jit(solution)/shard_map/while/body/eval_jaxpr/mul | solution.py:74
  124.5 4.0 %convolution_add_fusion.2 = f32[128,2048]{1,0:T(8,128)S(1)} fusion(bf16[1024,2048]{0,1:T(8,128)(2,1)} %bitcast.56, f32[128,2048]{1,0:T(8,128)S(1)} %get-tuple-element.306, pred[]{:T(512)S(6)} %compare.16, bf16[4096,128]{1,0:T(8,128)(2,1)} %get-tuple-element.316, s32[]{:T(128)S(6)} %select_n.65), kind=kOutput, calls=%fused_computation.2.clone.1 | convolution fusion | flops 537395200 | bytes 6553605 | tf_op jit(solution)/shard_map/while/body/eval_jaxpr/dot_general | solution.py:75
  129.4 2.2 %broadcast_multiply_fusion.2 = bf16[1024,32,64]{0,2,1:T(8,128)(2,1)} fusion(bf16[1024,64]{0,1:T(8,128)(2,1)S(1)} %constant_dynamic-slice_fusion.4, bf16[1024,32]{0,1:T(8,128)(2,1)S(1)} %constant_dynamic-slice_fusion.5), kind=kLoop, calls=%fused_computation.3.clone.1 | loop fusion | flops 2097152 | bytes 4390912 | tf_op jit(solution)/shard_map/while/body/eval_jaxpr/mul | solution.py:74
  131.7 4.0 %convolution_add_fusion.2 = f32[128,2048]{1,0:T(8,128)S(1)} fusion(bf16[1024,2048]{0,1:T(8,128)(2,1)} %bitcast.56, f32[128,2048]{1,0:T(8,128)S(1)} %get-tuple-element.306, pred[]{:T(512)S(6)} %compare.16, bf16[4096,128]{1,0:T(8,128)(2,1)} %get-tuple-element.316, s32[]{:T(128)S(6)} %select_n.65), kind=kOutput, calls=%fused_computation.2.clone.1 | convolution fusion | flops 537395200 | bytes 6553605 | tf_op jit(solution)/shard_map/while/body/eval_jaxpr/dot_general | solution.py:75
  139.6 1.9 %fusion.3 = bf16[32,128,64]{1,2,0:T(8,128)(2,1)} fusion(f32[128,32,64]{0,2,1:T(8,128)S(1)} %bitcast.66, f32[64,64]{1,0:T(8,128)S(1)} %copy-done.2), kind=kOutput, calls=%fused_computation.10 | convolution fusion | flops 201588736 | bytes 1589248 | tf_op jit(solution)/shard_map/dot_general | solution.py:26
  141.5 2.4 %copy.30 = bf16[32,128,64]{2,1,0:T(8,128)(2,1)} copy(bf16[32,128,64]{1,2,0:T(8,128)(2,1)} %fusion.3) | data formatting | bytes 1048576 | tf_op jit(solution)/shard_map/convert_element_type | solution.py:33
  143.9 2.7 %convert_element_type.24 = bf16[32,8192]{1,0:T(8,128)(2,1)} reshape(bf16[32,128,64]{2,1,0:T(8,128)(2,1)} %copy.30) | data formatting | bytes 1048576 | tf_op jit(solution)/shard_map/convert_element_type | solution.py:33
  146.6 32.4 %while.28 = (s32[]{:T(128)}, bf16[32,8192]{1,0:T(8,128)(2,1)}, bf16[128,192]{1,0:T(8,128)(2,1)S(1)}, bf16[192,8192]{1,0:T(8,128)(2,1)S(1)}, s32[3]{0:T(128)S(1)}...) while((s32[]{:T(128)}, bf16[32,8192]{1,0:T(8,128)(2,1)}, ...), condition=%wide.region_3.4_spmd, body=%wide.region_2.3_spmd.sunk | while | flops 100669456 | bytes 6832468 | solution.py:94
  146.6 1.9 %copy.51 = bf16[32,8192]{1,0:T(8,128)(2,1)} copy(bf16[32,8192]{1,0:T(8,128)(2,1)} %get-tuple-element.336) | data formatting | bytes 1048576 | tf_op jit(solution)/shard_map
  149.7 2.1 %fusion.31 = bf16[128,192]{1,0:T(8,128)(2,1)S(1)} fusion(bf16[128,192]{1,0:T(8,128)(2,1)S(1)} %get-tuple-element.337, s32[]{:T(128)S(6)} %select_n.64, bf16[32,8192]{1,0:T(8,128)(2,1)} %copy.51, bf16[192,8192]{1,0:T(8,128)(2,1)S(1)} %get-tuple-element.350), kind=kOutput, calls=%fused_computation.1.clone.1 | convolution fusion | flops 100669440 | bytes 3686404 | tf_op jit(solution)/shard_map/while/body/eval_jaxpr/dot_general | solution.py:38
  151.8 5.6 %collective-permute-done = bf16[32,8192]{1,0:T(8,128)(2,1)} collective-permute-done((bf16[32,8192]{1,0:T(8,128)(2,1)}, bf16[32,8192]{1,0:T(8,128)(2,1)}, u32[]{:S(2)}, u32[]{:S(2)}) %collective-permute-start) | collective-permute-done | bytes 524320 | tf_op jit(solution)/shard_map/while/body/eval_jaxpr/ppermute | solution.py:13
  160.5 2.1 %fusion.31 = bf16[128,192]{1,0:T(8,128)(2,1)S(1)} fusion(bf16[128,192]{1,0:T(8,128)(2,1)S(1)} %get-tuple-element.337, s32[]{:T(128)S(6)} %select_n.64, bf16[32,8192]{1,0:T(8,128)(2,1)} %copy.51, bf16[192,8192]{1,0:T(8,128)(2,1)S(1)} %get-tuple-element.350), kind=kOutput, calls=%fused_computation.1.clone.1 | convolution fusion | flops 100669440 | bytes 3686404 | tf_op jit(solution)/shard_map/while/body/eval_jaxpr/dot_general | solution.py:38
  162.6 5.6 %collective-permute-done = bf16[32,8192]{1,0:T(8,128)(2,1)} collective-permute-done((bf16[32,8192]{1,0:T(8,128)(2,1)}, bf16[32,8192]{1,0:T(8,128)(2,1)}, u32[]{:S(2)}, u32[]{:S(2)}) %collective-permute-start) | collective-permute-done | bytes 524320 | tf_op jit(solution)/shard_map/while/body/eval_jaxpr/ppermute | solution.py:13
  171.2 2.1 %fusion.31 = bf16[128,192]{1,0:T(8,128)(2,1)S(1)} fusion(bf16[128,192]{1,0:T(8,128)(2,1)S(1)} %get-tuple-element.337, s32[]{:T(128)S(6)} %select_n.64, bf16[32,8192]{1,0:T(8,128)(2,1)} %copy.51, bf16[192,8192]{1,0:T(8,128)(2,1)S(1)} %get-tuple-element.350), kind=kOutput, calls=%fused_computation.1.clone.1 | convolution fusion | flops 100669440 | bytes 3686404 | tf_op jit(solution)/shard_map/while/body/eval_jaxpr/dot_general | solution.py:38
  173.4 5.6 %collective-permute-done = bf16[32,8192]{1,0:T(8,128)(2,1)} collective-permute-done((bf16[32,8192]{1,0:T(8,128)(2,1)}, bf16[32,8192]{1,0:T(8,128)(2,1)}, u32[]{:S(2)}, u32[]{:S(2)}) %collective-permute-start) | collective-permute-done | bytes 524320 | tf_op jit(solution)/shard_map/while/body/eval_jaxpr/ppermute | solution.py:13
  179.7 2.1 %fusion.4 = bf16[1,32,192]{2,1,0:T(8,128)(2,1)S(1)} fusion(bf16[32,8192]{1,0:T(8,128)(2,1)} %get-tuple-element.180, bf16[1,192,8192]{2,1,0:T(8,128)(2,1)S(1)} %bitcast.58), kind=kOutput, calls=%fused_computation.12 | convolution fusion | flops 100669440 | bytes 3682304 | tf_op jit(solution)/shard_map/dot_general | solution.py:38
  (47 shorter events, 21.5 us)
Async XLA Ops:
  0.0 135.7 %copy-start = (f32[128,128]{1,0:T(8,128)S(1)}, f32[128,128]{1,0:T(8,128)}, u32[]{:S(2)}) copy-start(f32[128,128]{1,0:T(8,128)} %param.22) | copy-start | bytes 196612
  1.4 36.5 %all-to-all-start.1 = ((s32[1,8,512]{2,0,1:T(1,128)}), s32[1,8,512]{2,0,1:T(1,128)S(1)}, u32[]{:S(2)}, u32[]{:S(2)}) async-start(s32[1,8,512]{2,0,1:T(1,128)} %bitcast.1), calls=%async_computation.1 | async-start | bytes 32768 | tf_op jit(solution)/shard_map/all_to_all | solution.py:55
  37.9 32.6 %all-to-all-start.2 = ((bf16[8,2,16384]{2,1,0:T(2,128)(2,1)}), bf16[8,2,16384]{2,1,0:T(2,128)(2,1)}, u32[]{:S(2)}, u32[]{:S(2)}) async-start(bf16[8,2,16384]{2,1,0:T(2,128)(2,1)} %reshape.110), calls=%async_computation.2 | async-start | bytes 1048576 | tf_op jit(solution)/shard_map/all_to_all | solution.py:53
  47.1 29.5 %copy-start.3 = (f32[64]{0:T(128)S(1)}, f32[64]{0:T(128)}, u32[]{:S(2)}) copy-start(f32[64]{0:T(128)} %param.19) | copy-start | bytes 772
  47.1 29.5 %copy-start.4 = (f32[128]{0:T(128)S(1)}, f32[128]{0:T(128)}, u32[]{:S(2)}) copy-start(f32[128]{0:T(128)} %param.20) | copy-start | bytes 1540
  47.1 29.6 %copy-start.5 = (s32[1,32]{1,0:T(1,128)S(1)}, s32[1,32]{1,0:T(1,128)}, u32[]{:S(2)}) copy-start(s32[1,32]{1,0:T(1,128)} %param.18) | copy-start | bytes 388
  70.6 31.0 %all-to-all-start = ((bf16[8,2,32768]{2,1,0:T(2,128)(2,1)}), bf16[8,2,32768]{2,1,0:T(2,128)(2,1)}, u32[]{:S(2)}, u32[]{:S(2)}) async-start(bf16[8,2,32768]{2,1,0:T(2,128)(2,1)} %reshape.108), calls=%async_computation | async-start | bytes 2097152 | tf_op jit(solution)/shard_map/all_to_all | solution.py:54
  107.0 30.5 %copy-start.2 = (f32[64,64]{1,0:T(8,128)S(1)}, f32[64,64]{1,0:T(8,128)}, u32[]{:S(2)}) copy-start(f32[64,64]{1,0:T(8,128)} %param.21) | copy-start | bytes 49156
  138.6 8.0 %copy-start.1 = (bf16[1,192,8192]{2,1,0:T(8,128)(2,1)S(1)}, bf16[1,192,8192]{2,1,0:T(8,128)(2,1)}, u32[]{:S(2)}) copy-start(bf16[1,192,8192]{2,1,0:T(8,128)(2,1)} %param.23) | copy-start | bytes 9437188
  148.5 8.9 %collective-permute-start = (bf16[32,8192]{1,0:T(8,128)(2,1)}, bf16[32,8192]{1,0:T(8,128)(2,1)}, u32[]{:S(2)}, u32[]{:S(2)}) collective-permute-start(bf16[32,8192]{1,0:T(8,128)(2,1)} %copy.51), channel_id=1, source_target_pairs={{0,1},{1,2},{2,3},{3,0},{4,5},{5,6},{6,7},{7,4},{8,9},{9,10},{10,1... | collective-permute-start | bytes 1572872 | tf_op jit(solution)/shard_map/while/body/eval_jaxpr/ppermute | solution.py:13
  159.3 8.9 %collective-permute-start = (bf16[32,8192]{1,0:T(8,128)(2,1)}, bf16[32,8192]{1,0:T(8,128)(2,1)}, u32[]{:S(2)}, u32[]{:S(2)}) collective-permute-start(bf16[32,8192]{1,0:T(8,128)(2,1)} %copy.51), channel_id=1, source_target_pairs={{0,1},{1,2},{2,3},{3,0},{4,5},{5,6},{6,7},{7,4},{8,9},{9,10},{10,1... | collective-permute-start | bytes 1572872 | tf_op jit(solution)/shard_map/while/body/eval_jaxpr/ppermute | solution.py:13
  170.1 8.9 %collective-permute-start = (bf16[32,8192]{1,0:T(8,128)(2,1)}, bf16[32,8192]{1,0:T(8,128)(2,1)}, u32[]{:S(2)}, u32[]{:S(2)}) collective-permute-start(bf16[32,8192]{1,0:T(8,128)(2,1)} %copy.51), channel_id=1, source_target_pairs={{0,1},{1,2},{2,3},{3,0},{4,5},{5,6},{6,7},{7,4},{8,9},{9,10},{10,1... | collective-permute-start | bytes 1572872 | tf_op jit(solution)/shard_map/while/body/eval_jaxpr/ppermute | solution.py:13
where the time goes:
time: 185 us; the launch traced here: 184 us
  other arithmetic  55.2 us (30%)
  local copies, waits for them, and re-layouts  43 us (23%)
  waiting for transfers between devices  33.7 us (18%)
  matrix products  30.1 us (16%)
  starting transfers between devices  19.3 us (10%)
  loops' own time  1.96 us (1%)
    unnamed x3, other arithmetic  44.6 us
    unnamed x20, local copies, waits for them, and re-layouts  20.8 us
    all_to_all x1, waiting for transfers between devices, on_device(): lax.all_to_all(out_rows, 'query', split_axis=1, concat_axis=1, tiled=True)  16.9 us
    ppermute x3, waiting for transfers between devices, from_behind(): lax.ppermute(x, axis, [(i, (i + by) % devices) for i in range(devices)])  16.9 us
    dot_general x4, matrix products, accumulate(): lax.dot_general(g_part, spread, (((0,), (0,)), ((), ())), preferred_eleme...  15.9 us
    mul x4, other arithmetic, accumulate(): w_part[:, :, None] * x_part[:, None, :]  8.93 us
    dot_general x4, matrix products, record(): lax.dot_general(query_block, train_slab, (((1,), (1,)), ((), ())), prefer...  8.42 us
    all_to_all x1, starting transfers between devices, on_device(): lax.all_to_all(packed_keys, 'query', split_axis=1, concat_axis=1, tiled=T...  7.31 us
  transfers between devices with their start and end apart: 6, of which 4 were waited for; matrix products, arithmetic and copies ran while one was open for 39% of the time, Pallas kernels for 0%

commit v1 on v0

--- a/solution.py
+++ b/solution.py
@@ -6,6 +6,22 @@
 
 damping = 0.1
 highest = lax.Precision.HIGHEST
+
+
+def pairwise_exchange(array, axis, split, join):
+    ways, here = (lax.axis_size(axis), lax.axis_index(axis))
+    width = array.shape[split] // ways
+    lengths = list(array.shape)
+    lengths[split] = width
+    height = lengths[join]
+    lengths[join] = height * ways
+    full = jnp.zeros(lengths, array.dtype)
+    for mask in range(ways):
+        part = lax.dynamic_slice_in_dim(array, (here ^ mask) * width, width, axis=split)
+        if mask:
+            part = lax.ppermute(part, axis, [(d, d ^ mask) for d in range(ways)])
+        full = lax.dynamic_update_slice_in_dim(full, part, (here ^ mask) * height, axis=join)
+    return full
 
 
 def from_behind(x, axis, by):
@@ -50,7 +66,7 @@
     in_width = in_rows.shape[2]
     packed_keys = row_doc * 65536 + row_pos
     inputs_side, grads_side, keys_side = (
-        lax.all_to_all(in_rows, "query", split_axis=1, concat_axis=1, tiled=True),
+        pairwise_exchange(in_rows, "query", 1, 1),
         lax.all_to_all(out_rows, "query", split_axis=1, concat_axis=1, tiled=True),
         lax.all_to_all(packed_keys, "query", split_axis=1, concat_axis=1, tiled=True),
     )

time: 185 us -> 170 us (0.919)
  other arithmetic: 55.2 us -> 34.5 us
  starting transfers between devices: 19.3 us -> 25.1 us
    unnamed x3 -> x2, other arithmetic: 44.6 us -> 23.3 us
    ppermute x0 -> x7, waiting for transfers between devices: none -> 18.1 us  [pairwise_exchange(): part = lax.ppermute(part, axis, [(d, d ^ mask) for d in range(ways)])]
    all_to_all x1, waiting for transfers between devices: 16.9 us -> 0.01 us  [on_device(): lax.all_to_all(out_rows, 'query', split_axis=1, concat_axis=1, tiled=True)]
    ppermute x0 -> x7, starting transfers between devices: none -> 15.3 us  [pairwise_exchange(): part = lax.ppermute(part, axis, [(d, d ^ mask) for d in range(ways)])]
    unnamed x20 -> x19, local copies, waits for them, and re-layouts: 20.8 us -> 11.3 us
    dynamic_update_slice x0 -> x8, local copies, waits for them, and re-layouts: none -> 9.33 us  [pairwise_exchange(): lax.dynamic_update_slice_in_dim(full, part, (here ^ mask) * height, axis=...]
    all_to_all x1 -> x0, starting transfers between devices: 5.99 us -> none  [on_device(): lax.all_to_all(in_rows, 'query', split_axis=1, concat_axis=1, tiled=True)]
    all_to_all x1 -> x0, local copies, waits for them, and re-layouts: 3.63 us -> none  [on_device(): lax.all_to_all(in_rows, 'query', split_axis=1, concat_axis=1, tiled=True)]
  transfers between devices with their start and end apart: 6 -> 12, of which waited for: 4 -> 4; matrix products, arithmetic and copies ran while one was open for 39% -> 29% of each run, Pallas kernels for 0% -> 0%
where the time goes in v1:
time: 170 us; the launch traced here: 169 us
  local copies, waits for them, and re-layouts  42 us (25%)
  waiting for transfers between devices  34.8 us (20%)
  other arithmetic  34.5 us (20%)
  matrix products  30.1 us (18%)
  starting transfers between devices  25.1 us (15%)
  loops' own time  2.17 us (1%)
    unnamed x2, other arithmetic  23.3 us
    ppermute x7, waiting for transfers between devices, pairwise_exchange(): part = lax.ppermute(part, axis, [(d, d ^ mask) for d in range(ways)])  18.1 us
    ppermute x3, waiting for transfers between devices, from_behind(): lax.ppermute(x, axis, [(i, (i + by) % devices) for i in range(devices)])  16.7 us
    dot_general x4, matrix products, accumulate(): lax.dot_general(g_part, spread, (((0,), (0,)), ((), ())), preferred_eleme...  15.9 us
    ppermute x7, starting transfers between devices, pairwise_exchange(): part = lax.ppermute(part, axis, [(d, d ^ mask) for d in range(ways)])  15.3 us
    unnamed x19, local copies, waits for them, and re-layouts  11.3 us
    dynamic_update_slice x8, local copies, waits for them, and re-layouts, pairwise_exchange(): lax.dynamic_update_slice_in_dim(full, part, (here ^ mask) * height, axis=...  9.33 us
    mul x4, other arithmetic, accumulate(): w_part[:, :, None] * x_part[:, None, :]  8.93 us
  transfers between devices with their start and end apart: 12, of which 4 were waited for; matrix products, arithmetic and copies ran while one was open for 29% of the time, Pallas kernels for 0%

profile of v1, /device:TPU:0, one launch (start us, length us, event | category | flops | bytes accessed | tf_op | source)
XLA Modules:
  0.0 168.8 jit_solution(12254332946562195647)
XLA Ops:
  1.9 3.0 %collective-permute-start.1 = (bf16[1,512,64]{1,2,0:T(8,128)(2,1)}, bf16[1,512,64]{1,2,0:T(8,128)(2,1)}, u32[]{:S(2)}, u32[]{:S(2)}) collective-permute-start(bf16[1,512,64]{1,2,0:T(8,128)(2,1)} %get-tuple-element.226), channel_id=1, source_target_pairs={{0,4},{4,0},{8,12},{12,8},{16,20},{20,16},{24,28},{28,24},{1,5},{5... | collective-permute-start | bytes 196616 | tf_op jit(solution)/shard_map/ppermute | solution.py:22
  6.4 3.0 %collective-permute-start.4 = (bf16[1,512,64]{1,2,0:T(8,128)(2,1)}, bf16[1,512,64]{1,2,0:T(8,128)(2,1)}, u32[]{:S(2)}, u32[]{:S(2)}) collective-permute-start(bf16[1,512,64]{1,2,0:T(8,128)(2,1)} %get-tuple-element.223), channel_id=1, source_target_pairs={{0,16},{4,20},{8,24},{12,28},{16,0},{20,4},{24,8},{28,12},{1,17},{... | collective-permute-start | bytes 196616 | tf_op jit(solution)/shard_map/ppermute | solution.py:22
  10.8 3.8 %all-to-all-start.1 = ((s32[1,8,512]{2,0,1:T(1,128)}), s32[1,8,512]{2,0,1:T(1,128)S(1)}, u32[]{:S(2)}, u32[]{:S(2)}) async-start(s32[1,8,512]{2,0,1:T(1,128)} %bitcast.1), calls=%async_computation.1 | async-start | bytes 32768 | tf_op jit(solution)/shard_map/all_to_all | solution.py:71
  17.7 3.2 %copy.42 = bf16[1,4096,128]{2,0,1:T(2,128)(2,1)S(1)} copy(bf16[1,4096,128]{2,1,0:T(8,128)(2,1)} %param.15) | data formatting | bytes 2097152 | tf_op args[1]
  21.4 23.3 %reduce = bf16[4096,128]{1,0:T(8,128)(2,1)} reduce(bf16[4096,1,128]{2,1,0:T(2,128)(2,1)S(1)} %bitcast.73, bf16[]{:T(256)} %broadcast.102), dimensions={1}, to_apply=%bitcast.58.reduce_sub_computation | reduce | bytes 2097154
  44.7 2.2 %reshape.124 = bf16[8,2,32768]{2,1,0:T(2,128)(2,1)} reshape(bf16[4096,128]{1,0:T(8,128)(2,1)} %reduce) | data formatting | bytes 2097152
  46.9 6.0 %all-to-all-start = ((bf16[8,2,32768]{2,1,0:T(2,128)(2,1)}), bf16[8,2,32768]{2,1,0:T(2,128)(2,1)}, u32[]{:S(2)}, u32[]{:S(2)}) async-start(bf16[8,2,32768]{2,1,0:T(2,128)(2,1)} %reshape.124), calls=%async_computation | async-start | bytes 2097152 | tf_op jit(solution)/shard_map/all_to_all | solution.py:70
  53.1 3.9 %collective-permute-start.5 = (bf16[1,512,64]{1,2,0:T(8,128)(2,1)S(1)}, bf16[1,512,64]{1,2,0:T(8,128)(2,1)S(1)}, u32[]{:S(2)}, u32[]{:S(2)}) collective-permute-start(bf16[1,512,64]{1,2,0:T(8,128)(2,1)S(1)} %copy-done.5), channel_id=1, source_target_pairs={{0,20},{4,16},{8,28},{12,24},{16,4},{20,0},{24,12},{28,8},{1,21},{... | collective-permute-start | bytes 196616 | tf_op jit(solution)/shard_map/ppermute | solution.py:22
  61.4 2.4 %collective-permute-start.7 = (bf16[1,512,64]{1,2,0:T(8,128)(2,1)S(1)}, bf16[1,512,64]{1,2,0:T(8,128)(2,1)S(1)}, u32[]{:S(2)}, u32[]{:S(2)}) collective-permute-start(bf16[1,512,64]{1,2,0:T(8,128)(2,1)S(1)} %copy-done.3), channel_id=1, source_target_pairs={{0,28},{4,24},{8,20},{12,16},{16,12},{20,8},{24,4},{28,0},{1,29},{... | collective-permute-start | bytes 196616 | tf_op jit(solution)/shard_map/ppermute | solution.py:22
  66.7 18.1 %collective-permute-done.5 = bf16[1,512,64]{1,2,0:T(8,128)(2,1)S(1)} collective-permute-done((bf16[1,512,64]{1,2,0:T(8,128)(2,1)S(1)}, bf16[1,512,64]{1,2,0:T(8,128)(2,1)S(1)}, u32[]{:S(2)}, u32[]{:S(2)}) %collective-permute-start.5) | collective-permute-done | bytes 65568 | tf_op jit(solution)/shard_map/ppermute | solution.py:22
  86.8 4.3 %reshape.125 = bf16[4096,1,128]{2,1,0:T(2,128)(2,1)S(1)} reshape(bf16[8,2,32768]{2,1,0:T(2,128)(2,1)} %all-to-all-done) | data formatting | bytes 2097152
  92.2 28.7 %while.29 = (s32[]{:T(128)}, f32[128,2048]{1,0:T(8,128)S(1)}, bf16[4096,128]{1,0:T(8,128)(2,1)}, bf16[4096,32]{0,1:T(8,128)(2,1)S(1)}, bf16[4096,64]{0,1:T(8,128...) while((s32[]{:T(128)}, f32[128,2048]{1,0:T(8,128)S(1)}, bf16[4096,128]{1,0:T(8,128)(2,1)}, ...), condition=%wide.region_1.2_spmd.clone, body=%wide.region_0.1_spmd.clone.sunk | while | flops 539492352 | bytes 11337889 | solution.py:96
  93.1 2.2 %broadcast_multiply_fusion.2 = bf16[1024,32,64]{0,2,1:T(8,128)(2,1)} fusion(bf16[1024,64]{0,1:T(8,128)(2,1)S(1)} %constant_dynamic-slice_fusion.11, bf16[1024,32]{0,1:T(8,128)(2,1)S(1)} %constant_dynamic-slice_fusion.12), kind=kLoop, calls=%fused_computation.3.clone.1 | loop fusion | flops 2097152 | bytes 4390912 | tf_op jit(solution)/shard_map/while/body/eval_jaxpr/mul | solution.py:90
  95.4 4.0 %convolution_add_fusion.2 = f32[128,2048]{1,0:T(8,128)S(1)} fusion(bf16[1024,2048]{0,1:T(8,128)(2,1)} %bitcast.69, f32[128,2048]{1,0:T(8,128)S(1)} %get-tuple-element.308, pred[]{:T(512)S(6)} %compare.16, bf16[4096,128]{1,0:T(8,128)(2,1)} %get-tuple-element.318, s32[]{:T(128)S(6)} %select_n.105), kind=kOutput, calls=%fused_computation.2.clone.1 | convolution fusion | flops 537395200 | bytes 6553605 | tf_op jit(solution)/shard_map/while/body/eval_jaxpr/dot_general | solution.py:91
  100.3 2.2 %broadcast_multiply_fusion.2 = bf16[1024,32,64]{0,2,1:T(8,128)(2,1)} fusion(bf16[1024,64]{0,1:T(8,128)(2,1)S(1)} %constant_dynamic-slice_fusion.11, bf16[1024,32]{0,1:T(8,128)(2,1)S(1)} %constant_dynamic-slice_fusion.12), kind=kLoop, calls=%fused_computation.3.clone.1 | loop fusion | flops 2097152 | bytes 4390912 | tf_op jit(solution)/shard_map/while/body/eval_jaxpr/mul | solution.py:90
  102.6 4.0 %convolution_add_fusion.2 = f32[128,2048]{1,0:T(8,128)S(1)} fusion(bf16[1024,2048]{0,1:T(8,128)(2,1)} %bitcast.69, f32[128,2048]{1,0:T(8,128)S(1)} %get-tuple-element.308, pred[]{:T(512)S(6)} %compare.16, bf16[4096,128]{1,0:T(8,128)(2,1)} %get-tuple-element.318, s32[]{:T(128)S(6)} %select_n.105), kind=kOutput, calls=%fused_computation.2.clone.1 | convolution fusion | flops 537395200 | bytes 6553605 | tf_op jit(solution)/shard_map/while/body/eval_jaxpr/dot_general | solution.py:91
  107.5 2.2 %broadcast_multiply_fusion.2 = bf16[1024,32,64]{0,2,1:T(8,128)(2,1)} fusion(bf16[1024,64]{0,1:T(8,128)(2,1)S(1)} %constant_dynamic-slice_fusion.11, bf16[1024,32]{0,1:T(8,128)(2,1)S(1)} %constant_dynamic-slice_fusion.12), kind=kLoop, calls=%fused_computation.3.clone.1 | loop fusion | flops 2097152 | bytes 4390912 | tf_op jit(solution)/shard_map/while/body/eval_jaxpr/mul | solution.py:90
  109.7 4.0 %convolution_add_fusion.2 = f32[128,2048]{1,0:T(8,128)S(1)} fusion(bf16[1024,2048]{0,1:T(8,128)(2,1)} %bitcast.69, f32[128,2048]{1,0:T(8,128)S(1)} %get-tuple-element.308, pred[]{:T(512)S(6)} %compare.16, bf16[4096,128]{1,0:T(8,128)(2,1)} %get-tuple-element.318, s32[]{:T(128)S(6)} %select_n.105), kind=kOutput, calls=%fused_computation.2.clone.1 | convolution fusion | flops 537395200 | bytes 6553605 | tf_op jit(solution)/shard_map/while/body/eval_jaxpr/dot_general | solution.py:91
  114.7 2.2 %broadcast_multiply_fusion.2 = bf16[1024,32,64]{0,2,1:T(8,128)(2,1)} fusion(bf16[1024,64]{0,1:T(8,128)(2,1)S(1)} %constant_dynamic-slice_fusion.11, bf16[1024,32]{0,1:T(8,128)(2,1)S(1)} %constant_dynamic-slice_fusion.12), kind=kLoop, calls=%fused_computation.3.clone.1 | loop fusion | flops 2097152 | bytes 4390912 | tf_op jit(solution)/shard_map/while/body/eval_jaxpr/mul | solution.py:90
  116.9 4.0 %convolution_add_fusion.2 = f32[128,2048]{1,0:T(8,128)S(1)} fusion(bf16[1024,2048]{0,1:T(8,128)(2,1)} %bitcast.69, f32[128,2048]{1,0:T(8,128)S(1)} %get-tuple-element.308, pred[]{:T(512)S(6)} %compare.16, bf16[4096,128]{1,0:T(8,128)(2,1)} %get-tuple-element.318, s32[]{:T(128)S(6)} %select_n.105), kind=kOutput, calls=%fused_computation.2.clone.1 | convolution fusion | flops 537395200 | bytes 6553605 | tf_op jit(solution)/shard_map/while/body/eval_jaxpr/dot_general | solution.py:91
  124.8 1.9 %fusion.3 = bf16[32,128,64]{1,2,0:T(8,128)(2,1)} fusion(f32[128,32,64]{0,2,1:T(8,128)S(1)} %bitcast.77, f32[64,64]{1,0:T(8,128)S(1)} %copy-done.2), kind=kOutput, calls=%fused_computation.10 | convolution fusion | flops 201588736 | bytes 1589248 | tf_op jit(solution)/shard_map/dot_general | solution.py:42
  126.7 2.4 %copy.33 = bf16[32,128,64]{2,1,0:T(8,128)(2,1)} copy(bf16[32,128,64]{1,2,0:T(8,128)(2,1)} %fusion.3) | data formatting | bytes 1048576 | tf_op jit(solution)/shard_map/convert_element_type | solution.py:49
  129.1 2.7 %convert_element_type.24 = bf16[32,8192]{1,0:T(8,128)(2,1)} reshape(bf16[32,128,64]{2,1,0:T(8,128)(2,1)} %copy.33) | data formatting | bytes 1048576 | tf_op jit(solution)/shard_map/convert_element_type | solution.py:49
  131.8 32.4 %while.28 = (s32[]{:T(128)}, bf16[32,8192]{1,0:T(8,128)(2,1)}, bf16[128,192]{1,0:T(8,128)(2,1)S(1)}, bf16[192,8192]{1,0:T(8,128)(2,1)S(1)}, s32[3]{0:T(128)S(1)}...) while((s32[]{:T(128)}, bf16[32,8192]{1,0:T(8,128)(2,1)}, ...), condition=%wide.region_3.4_spmd, body=%wide.region_2.3_spmd.sunk | while | flops 100669456 | bytes 6832468 | solution.py:110
  131.8 1.9 %copy.62 = bf16[32,8192]{1,0:T(8,128)(2,1)} copy(bf16[32,8192]{1,0:T(8,128)(2,1)} %get-tuple-element.338) | data formatting | bytes 1048576 | tf_op jit(solution)/shard_map
  135.0 2.1 %fusion.31 = bf16[128,192]{1,0:T(8,128)(2,1)S(1)} fusion(bf16[128,192]{1,0:T(8,128)(2,1)S(1)} %get-tuple-element.339, s32[]{:T(128)S(6)} %select_n.104, bf16[32,8192]{1,0:T(8,128)(2,1)} %copy.62, bf16[192,8192]{1,0:T(8,128)(2,1)S(1)} %get-tuple-element.352), kind=kOutput, calls=%fused_computation.1.clone.1 | convolution fusion | flops 100669440 | bytes 3686404 | tf_op jit(solution)/shard_map/while/body/eval_jaxpr/dot_general | solution.py:54
  137.1 5.6 %collective-permute-done = bf16[32,8192]{1,0:T(8,128)(2,1)} collective-permute-done((bf16[32,8192]{1,0:T(8,128)(2,1)}, bf16[32,8192]{1,0:T(8,128)(2,1)}, u32[]{:S(2)}, u32[]{:S(2)}) %collective-permute-start) | collective-permute-done | bytes 524320 | tf_op jit(solution)/shard_map/while/body/eval_jaxpr/ppermute | solution.py:29
  145.8 2.1 %fusion.31 = bf16[128,192]{1,0:T(8,128)(2,1)S(1)} fusion(bf16[128,192]{1,0:T(8,128)(2,1)S(1)} %get-tuple-element.339, s32[]{:T(128)S(6)} %select_n.104, bf16[32,8192]{1,0:T(8,128)(2,1)} %copy.62, bf16[192,8192]{1,0:T(8,128)(2,1)S(1)} %get-tuple-element.352), kind=kOutput, calls=%fused_computation.1.clone.1 | convolution fusion | flops 100669440 | bytes 3686404 | tf_op jit(solution)/shard_map/while/body/eval_jaxpr/dot_general | solution.py:54
  147.9 5.6 %collective-permute-done = bf16[32,8192]{1,0:T(8,128)(2,1)} collective-permute-done((bf16[32,8192]{1,0:T(8,128)(2,1)}, bf16[32,8192]{1,0:T(8,128)(2,1)}, u32[]{:S(2)}, u32[]{:S(2)}) %collective-permute-start) | collective-permute-done | bytes 524320 | tf_op jit(solution)/shard_map/while/body/eval_jaxpr/ppermute | solution.py:29
  156.5 2.1 %fusion.31 = bf16[128,192]{1,0:T(8,128)(2,1)S(1)} fusion(bf16[128,192]{1,0:T(8,128)(2,1)S(1)} %get-tuple-element.339, s32[]{:T(128)S(6)} %select_n.104, bf16[32,8192]{1,0:T(8,128)(2,1)} %copy.62, bf16[192,8192]{1,0:T(8,128)(2,1)S(1)} %get-tuple-element.352), kind=kOutput, calls=%fused_computation.1.clone.1 | convolution fusion | flops 100669440 | bytes 3686404 | tf_op jit(solution)/shard_map/while/body/eval_jaxpr/dot_general | solution.py:54
  158.6 5.6 %collective-permute-done = bf16[32,8192]{1,0:T(8,128)(2,1)} collective-permute-done((bf16[32,8192]{1,0:T(8,128)(2,1)}, bf16[32,8192]{1,0:T(8,128)(2,1)}, u32[]{:S(2)}, u32[]{:S(2)}) %collective-permute-start) | collective-permute-done | bytes 524320 | tf_op jit(solution)/shard_map/while/body/eval_jaxpr/ppermute | solution.py:29
  164.2 2.1 %fusion.4 = bf16[1,32,192]{2,1,0:T(8,128)(2,1)S(1)} fusion(bf16[32,8192]{1,0:T(8,128)(2,1)} %get-tuple-element.180, bf16[1,192,8192]{2,1,0:T(8,128)(2,1)S(1)} %bitcast.71), kind=kOutput, calls=%fused_computation.12 | convolution fusion | flops 100669440 | bytes 3682304 | tf_op jit(solution)/shard_map/dot_general | solution.py:54
  (66 shorter events, 34.5 us)
Async XLA Ops:
  0.0 120.9 %copy-start = (f32[128,128]{1,0:T(8,128)S(1)}, f32[128,128]{1,0:T(8,128)}, u32[]{:S(2)}) copy-start(f32[128,128]{1,0:T(8,128)} %param.22) | copy-start | bytes 196612
  1.9 55.1 %collective-permute-start.1 = (bf16[1,512,64]{1,2,0:T(8,128)(2,1)}, bf16[1,512,64]{1,2,0:T(8,128)(2,1)}, u32[]{:S(2)}, u32[]{:S(2)}) collective-permute-start(bf16[1,512,64]{1,2,0:T(8,128)(2,1)} %get-tuple-element.226), channel_id=1, source_target_pairs={{0,4},{4,0},{8,12},{12,8},{16,20},{20,16},{24,28},{28,24},{1,5},{5... | collective-permute-start | bytes 196616 | tf_op jit(solution)/shard_map/ppermute | solution.py:22
  4.9 55.0 %collective-permute-start.2 = (bf16[1,512,64]{1,2,0:T(8,128)(2,1)}, bf16[1,512,64]{1,2,0:T(8,128)(2,1)}, u32[]{:S(2)}, u32[]{:S(2)}) collective-permute-start(bf16[1,512,64]{1,2,0:T(8,128)(2,1)} %get-tuple-element.225), channel_id=1, source_target_pairs={{0,8},{4,12},{8,0},{12,4},{16,24},{20,28},{24,16},{28,20},{1,9},{5... | collective-permute-start | bytes 196616 | tf_op jit(solution)/shard_map/ppermute | solution.py:22
  6.4 57.3 %collective-permute-start.3 = (bf16[1,512,64]{1,2,0:T(8,128)(2,1)}, bf16[1,512,64]{1,2,0:T(8,128)(2,1)}, u32[]{:S(2)}, u32[]{:S(2)}) collective-permute-start(bf16[1,512,64]{1,2,0:T(8,128)(2,1)} %get-tuple-element.224), channel_id=1, source_target_pairs={{0,12},{4,8},{8,4},{12,0},{16,28},{20,24},{24,20},{28,16},{1,13},{... | collective-permute-start | bytes 196616 | tf_op jit(solution)/shard_map/ppermute | solution.py:22
  6.4 58.8 %collective-permute-start.4 = (bf16[1,512,64]{1,2,0:T(8,128)(2,1)}, bf16[1,512,64]{1,2,0:T(8,128)(2,1)}, u32[]{:S(2)}, u32[]{:S(2)}) collective-permute-start(bf16[1,512,64]{1,2,0:T(8,128)(2,1)} %get-tuple-element.223), channel_id=1, source_target_pairs={{0,16},{4,20},{8,24},{12,28},{16,0},{20,4},{24,8},{28,12},{1,17},{... | collective-permute-start | bytes 196616 | tf_op jit(solution)/shard_map/ppermute | solution.py:22
  10.8 36.1 %all-to-all-start.1 = ((s32[1,8,512]{2,0,1:T(1,128)}), s32[1,8,512]{2,0,1:T(1,128)S(1)}, u32[]{:S(2)}, u32[]{:S(2)}) async-start(s32[1,8,512]{2,0,1:T(1,128)} %bitcast.1), calls=%async_computation.1 | async-start | bytes 32768 | tf_op jit(solution)/shard_map/all_to_all | solution.py:71
  21.4 31.5 %copy-start.6 = (s32[1,32]{1,0:T(1,128)S(1)}, s32[1,32]{1,0:T(1,128)}, u32[]{:S(2)}) copy-start(s32[1,32]{1,0:T(1,128)} %param.18) | copy-start | bytes 388
  44.7 8.4 %copy-start.5 = (bf16[1,512,64]{1,2,0:T(8,128)(2,1)S(1)}, bf16[1,512,64]{1,2,0:T(8,128)(2,1)}, u32[]{:S(2)}) copy-start(bf16[1,512,64]{1,2,0:T(8,128)(2,1)} %get-tuple-element.222) | copy-start | bytes 196612
  44.7 13.8 %copy-start.4 = (bf16[1,512,64]{1,2,0:T(8,128)(2,1)S(1)}, bf16[1,512,64]{1,2,0:T(8,128)(2,1)}, u32[]{:S(2)}) copy-start(bf16[1,512,64]{1,2,0:T(8,128)(2,1)} %get-tuple-element.227) | copy-start | bytes 196612
  44.7 16.7 %copy-start.3 = (bf16[1,512,64]{1,2,0:T(8,128)(2,1)S(1)}, bf16[1,512,64]{1,2,0:T(8,128)(2,1)}, u32[]{:S(2)}) copy-start(bf16[1,512,64]{1,2,0:T(8,128)(2,1)} %get-tuple-element.221) | copy-start | bytes 196612
  46.9 39.9 %all-to-all-start = ((bf16[8,2,32768]{2,1,0:T(2,128)(2,1)}), bf16[8,2,32768]{2,1,0:T(2,128)(2,1)}, u32[]{:S(2)}, u32[]{:S(2)}) async-start(bf16[8,2,32768]{2,1,0:T(2,128)(2,1)} %reshape.124), calls=%async_computation | async-start | bytes 2097152 | tf_op jit(solution)/shard_map/all_to_all | solution.py:70
  53.1 31.8 %collective-permute-start.5 = (bf16[1,512,64]{1,2,0:T(8,128)(2,1)S(1)}, bf16[1,512,64]{1,2,0:T(8,128)(2,1)S(1)}, u32[]{:S(2)}, u32[]{:S(2)}) collective-permute-start(bf16[1,512,64]{1,2,0:T(8,128)(2,1)S(1)} %copy-done.5), channel_id=1, source_target_pairs={{0,20},{4,16},{8,28},{12,24},{16,4},{20,0},{24,12},{28,8},{1,21},{... | collective-permute-start | bytes 196616 | tf_op jit(solution)/shard_map/ppermute | solution.py:22
  58.5 27.0 %collective-permute-start.6 = (bf16[1,512,64]{1,2,0:T(8,128)(2,1)S(1)}, bf16[1,512,64]{1,2,0:T(8,128)(2,1)S(1)}, u32[]{:S(2)}, u32[]{:S(2)}) collective-permute-start(bf16[1,512,64]{1,2,0:T(8,128)(2,1)S(1)} %copy-done.4), channel_id=1, source_target_pairs={{0,24},{4,28},{8,16},{12,20},{16,8},{20,12},{24,0},{28,4},{1,25},{... | collective-permute-start | bytes 196616 | tf_op jit(solution)/shard_map/ppermute | solution.py:22
  61.4 24.8 %collective-permute-start.7 = (bf16[1,512,64]{1,2,0:T(8,128)(2,1)S(1)}, bf16[1,512,64]{1,2,0:T(8,128)(2,1)S(1)}, u32[]{:S(2)}, u32[]{:S(2)}) collective-permute-start(bf16[1,512,64]{1,2,0:T(8,128)(2,1)S(1)} %copy-done.3), channel_id=1, source_target_pairs={{0,28},{4,24},{8,20},{12,16},{16,12},{20,8},{24,4},{28,0},{1,29},{... | collective-permute-start | bytes 196616 | tf_op jit(solution)/shard_map/ppermute | solution.py:22
  92.2 30.5 %copy-start.2 = (f32[64,64]{1,0:T(8,128)S(1)}, f32[64,64]{1,0:T(8,128)}, u32[]{:S(2)}) copy-start(f32[64,64]{1,0:T(8,128)} %param.21) | copy-start | bytes 49156
  123.8 8.0 %copy-start.1 = (bf16[1,192,8192]{2,1,0:T(8,128)(2,1)S(1)}, bf16[1,192,8192]{2,1,0:T(8,128)(2,1)}, u32[]{:S(2)}) copy-start(bf16[1,192,8192]{2,1,0:T(8,128)(2,1)} %param.23) | copy-start | bytes 9437188
  133.7 8.9 %collective-permute-start = (bf16[32,8192]{1,0:T(8,128)(2,1)}, bf16[32,8192]{1,0:T(8,128)(2,1)}, u32[]{:S(2)}, u32[]{:S(2)}) collective-permute-start(bf16[32,8192]{1,0:T(8,128)(2,1)} %copy.62), channel_id=1, source_target_pairs={{0,1},{1,2},{2,3},{3,0},{4,5},{5,6},{6,7},{7,4},{8,9},{9,10},{10,1... | collective-permute-start | bytes 1572872 | tf_op jit(solution)/shard_map/while/body/eval_jaxpr/ppermute | solution.py:29
  144.5 8.9 %collective-permute-start = (bf16[32,8192]{1,0:T(8,128)(2,1)}, bf16[32,8192]{1,0:T(8,128)(2,1)}, u32[]{:S(2)}, u32[]{:S(2)}) collective-permute-start(bf16[32,8192]{1,0:T(8,128)(2,1)} %copy.62), channel_id=1, source_target_pairs={{0,1},{1,2},{2,3},{3,0},{4,5},{5,6},{6,7},{7,4},{8,9},{9,10},{10,1... | collective-permute-start | bytes 1572872 | tf_op jit(solution)/shard_map/while/body/eval_jaxpr/ppermute | solution.py:29
  155.3 8.9 %collective-permute-start = (bf16[32,8192]{1,0:T(8,128)(2,1)}, bf16[32,8192]{1,0:T(8,128)(2,1)}, u32[]{:S(2)}, u32[]{:S(2)}) collective-permute-start(bf16[32,8192]{1,0:T(8,128)(2,1)} %copy.62), channel_id=1, source_target_pairs={{0,1},{1,2},{2,3},{3,0},{4,5},{5,6},{6,7},{7,4},{8,9},{9,10},{10,1... | collective-permute-start | bytes 1572872 | tf_op jit(solution)/shard_map/while/body/eval_jaxpr/ppermute | solution.py:29
